TPU v7x, 32 devices: a whole 2x2x4 slice. The times are simulated.
32 devices in a mesh: head: 4 (over y, x), pb: 8 (over z, core).
Axes of the slice: x: 2, y: 2, z: 4, core: 2. Of those that a mesh axis runs over, the one named last changes fastest.
Arguments:
- pair: bfloat16 [512, 512, 128], P('pb', 'head'), may hold values from -6 to 6
- tokens: bfloat16 [512, 768], P('pb'), may hold values from -6 to 6
- token_mask: int32 [512], replicated, may hold values from 0 to 1, as said below
- w_gu: bfloat16 [2, 128, 512], replicated, may hold values from -0.5 to 0.5
- w_down: bfloat16 [2, 256, 128], replicated, may hold values from -0.375 to 0.375
- w_bias: bfloat16 [128, 32], replicated, may hold values from -0.5 to 0.5
- w_q: bfloat16 [2, 768, 768], P(None, None, 'head'), may hold values from -0.21875 to 0.21875
- w_k: bfloat16 [2, 768, 768], P(None, None, 'head'), may hold values from -0.21875 to 0.21875
- w_v: bfloat16 [2, 768, 768], P(None, None, 'head'), may hold values from -0.21875 to 0.21875
- w_gate: bfloat16 [2, 768, 768], P(None, None, 'head'), may hold values from -0.21875 to 0.21875
- w_out: bfloat16 [2, 768, 768], P(None, 'head'), may hold values from -0.875 to 0.875
Outputs:
- updated: bfloat16 [512, 768], P('pb')
Inputs may be any that keep to these rules, and one draw needn't show every extreme that they name: `token_mask`: ones on a prefix of the tokens and zeros after it; at least 128 ones and at least one zero.
All inputs are finite; a program needn't handle non-finite values.
Results may differ from a plain program's by a relative error of at most 0.019.
Values may be sent and summed in bfloat16 or wider, within the bound.
A program may use at most 64 MiB of HBM per device.

v0:
```python
import math
import jax
import jax.numpy as jnp
from jax import lax
from jax.sharding import PartitionSpec as P

TRANS = 2
LAYERS = 2
HD = 48


def normalize(values):
    values = values.astype(jnp.float32)
    center = values - jnp.mean(values, axis=-1, keepdims=True)
    spread = jnp.mean(center * center, axis=-1, keepdims=True)
    return center * lax.rsqrt(spread + 1e-05)


def transition(pair_rows, w_updown, w_back):
    hidden_units = w_back.shape[0]
    normed = normalize(pair_rows).astype(jnp.bfloat16)
    mixed = jnp.dot(normed, w_updown, preferred_element_type=jnp.float32)
    hidden = (jax.nn.silu(mixed[:, :hidden_units]) * mixed[:, hidden_units:]).astype(jnp.bfloat16)
    summed = pair_rows.astype(jnp.float32) + jnp.dot(
        hidden, w_back, preferred_element_type=jnp.float32
    )
    return summed.astype(jnp.bfloat16)


def on_device(pair, tokens, token_mask, w_gu, w_down, w_bias, w_q, w_k, w_v, w_gate, w_out):
    row_count, col_count, channels = pair.shape
    entries = row_count * col_count
    block_rows = math.gcd(entries, 2048)
    blocked = pair.reshape(entries // block_rows, block_rows, channels)
    heads_all = w_bias.shape[1] // LAYERS

    def project(pair_block):
        current = pair_block
        for section_index in range(TRANS):
            current = transition(current, w_gu[section_index], w_down[section_index])
        normed = normalize(current).astype(jnp.bfloat16)
        return jnp.einsum("rc,cj->jr", normed, w_bias, preferred_element_type=jnp.float32).astype(
            jnp.bfloat16
        )

    projected = lax.map(project, blocked)
    columns_first = jnp.transpose(projected, (1, 0, 2))
    bias_local = columns_first.reshape(LAYERS, heads_all, row_count, col_count)
    layer_bias = [
        lax.all_to_all(bias_local[layer_index], "head", split_axis=0, concat_axis=2, tiled=True)
        for layer_index in range(LAYERS)
    ]
    is_real = token_mask == 1
    query_real = lax.dynamic_slice_in_dim(
        token_mask, lax.axis_index("pb") * row_count, row_count, 0
    ).astype(jnp.float32)
    local_width = w_q.shape[2]
    local_heads = local_width // HD
    scale_factor = 1.0 / HD**0.5
    state = tokens.astype(jnp.float32)
    for layer_index in range(LAYERS):
        normed = normalize(state).astype(jnp.bfloat16)
        queries = jnp.dot(normed, w_q[layer_index], preferred_element_type=jnp.float32).astype(
            jnp.bfloat16
        )
        key_proj = jnp.dot(normed, w_k[layer_index], preferred_element_type=jnp.float32).astype(
            jnp.bfloat16
        )
        value_proj = jnp.dot(normed, w_v[layer_index], preferred_element_type=jnp.float32).astype(
            jnp.bfloat16
        )
        gate_vals = jnp.dot(normed, w_gate[layer_index], preferred_element_type=jnp.float32).astype(
            jnp.bfloat16
        )
        packed = jnp.concatenate([key_proj, value_proj], axis=1)
        query_heads = queries.astype(jnp.float32).reshape(row_count, local_heads, HD)
        bias_now = layer_bias[layer_index]
        every_key = lax.all_gather(packed, "pb", axis=0, tiled=True)
        piece_len = every_key.shape[0]
        key_heads = (
            every_key[:, :local_width].astype(jnp.float32).reshape(piece_len, local_heads, HD)
        )
        value_heads = (
            every_key[:, local_width:].astype(jnp.float32).reshape(piece_len, local_heads, HD)
        )
        scores = jnp.einsum("ihd,jhd->hij", query_heads, key_heads) * scale_factor
        scores = scores + bias_now.astype(jnp.float32)
        scores = jnp.where(is_real[None, None, :], scores, -1e30)
        old_peak = jnp.full((local_heads, row_count), -1e30, jnp.float32)
        new_peak = jnp.maximum(old_peak, jnp.max(scores, axis=-1))
        exp_scores = jnp.exp(scores - new_peak[..., None])
        new_total = jnp.sum(exp_scores, axis=-1)
        new_accum = jnp.einsum("hij,jhd->hid", exp_scores, value_heads)
        finished = (new_peak, new_total, new_accum)
        final_peak, final_total, final_accum = finished
        attended = jnp.transpose(final_accum / final_total[..., None], (1, 0, 2)).reshape(
            row_count, local_width
        )
        gated = (attended * jax.nn.sigmoid(gate_vals.astype(jnp.float32))).astype(jnp.bfloat16)
        partial_out = jnp.dot(gated, w_out[layer_index], preferred_element_type=jnp.float32)
        feature_share = lax.psum_scatter(
            partial_out.astype(jnp.bfloat16), "head", scatter_dimension=1, tiled=True
        ).astype(jnp.float32)
        share_width = feature_share.shape[1]
        own_features = lax.dynamic_slice_in_dim(
            state, lax.axis_index("head") * share_width, share_width, 1
        )
        state = lax.all_gather(
            (own_features + query_real[:, None] * feature_share).astype(jnp.bfloat16),
            "head",
            axis=1,
            tiled=True,
        ).astype(jnp.float32)
    return state.astype(jnp.bfloat16)


def solution(mesh):
    placed = (
        P("pb", "head", None),
        P("pb", None),
        P(),
        P(),
        P(),
        P(),
        P(None, None, "head"),
        P(None, None, "head"),
        P(None, None, "head"),
        P(None, None, "head"),
        P(None, "head", None),
    )
    return jax.shard_map(
        on_device, mesh=mesh, in_specs=placed, out_specs=P("pb", None), check_vma=False
    )
```

profile of v0, /device:TPU:0, one launch (start us, length us, event | category | flops | bytes accessed | tf_op | source)
XLA Modules:
  0.0 150.9 jit_solution(16466473360683681310)
XLA Ops:
  6.5 22.2 %while.10 = (s32[]{:T(128)}, bf16[4,32,2048]{2,1,0:T(8,128)(2,1)S(1)}, bf16[4,2048,128]{2,1,0:T(8,128)(2,1)}, bf16[2,128,512]{2,1,0:T(8,128)(2,1)}, bf16[2,256,1...) while((s32[]{:T(128)}, bf16[4,32,2048]{2,1,0:T(8,128)(2,1)S(1)}, ...), condition=%wide.region_9.10_spmd, body=%wide.region_2.9_spmd.sunk | while | flops 836573184 | bytes 30671024 | solution.py:46
  6.5 1.1 constant_dynamic-slice_fusion.2
  7.7 0.2 copy.71
  8.2 0.7 fusion.123
  8.9 0.2 copy-done.9
  9.1 0.8 fusion.124
  10.1 0.7 fusion.125
  10.8 0.8 fusion.126
  11.8 0.2 fusion.127
  12.1 1.1 constant_dynamic-slice_fusion.2
  13.2 0.2 copy.71
  13.7 0.7 fusion.123
  14.6 0.8 fusion.124
  15.6 0.7 fusion.125
  16.4 0.8 fusion.126
  17.4 0.2 fusion.127
  17.7 1.1 constant_dynamic-slice_fusion.2
  18.8 0.2 copy.71
  19.3 0.7 fusion.123
  20.2 0.8 fusion.124
  21.2 0.7 fusion.125
  22.0 0.8 fusion.126
  23.0 0.2 fusion.127
  23.2 1.1 constant_dynamic-slice_fusion.2
  24.3 0.2 copy.71
  24.9 0.7 fusion.123
  25.8 0.8 fusion.124
  26.8 0.7 fusion.125
  27.5 0.8 fusion.126
  28.5 0.2 fusion.127
  28.8 0.2 copy.49
  29.1 0.9 squeeze.53
  29.9 5.2 %all-to-all-start = ((bf16[16,64,128]{2,1,0:T(8,128)(2,1)}), bf16[16,64,128]{2,1,0:T(8,128)(2,1)S(1)}, u32[]{:S(2)}, u32[]{:S(2)}) async-start(bf16[16,64,128]{2,1,0:T(8,128)(2,1)} %squeeze.53), calls=%async_computation | async-start | bytes 524288 | tf_op jit(solution)/shard_map/all_to_all | solution.py:50
  35.2 0.2 multiply_reduce_fusion.3
  35.5 0.2 convolution_convert_fusion.8
  35.7 0.2 convolution_convert_fusion.9
  36.1 14.7 %all_gather.12 = bf16[512,384]{1,0:T(8,128)(2,1)S(1)} all-gather(bf16[64,384]{1,0:T(8,128)(2,1)S(1)} %pad_maximum_fusion), channel_id=1, replica_groups=mesh['head'=4,'pb'=8] {'pb'}, dimensions={0}, use_global_device_ids=true | all-gather | bytes 442368 | tf_op jit(solution)/shard_map/all_gather | solution.py:78
  51.1 0.2 convolution_convert_fusion.10
  51.7 0.4 fusion.95
  52.0 0.2 fusion.55
  52.3 0.3 fusion.40
  52.7 1.5 convolution_convert_fusion.2
  54.2 0.8 copy.61
  55.0 0.2 copy.56
  55.2 0.9 squeeze.59
  56.1 4.2 %all-to-all-start.1 = ((bf16[16,64,128]{2,1,0:T(8,128)(2,1)}), bf16[16,64,128]{2,1,0:T(8,128)(2,1)S(1)}, u32[]{:S(2)}, u32[]{:S(2)}) async-start(bf16[16,64,128]{2,1,0:T(8,128)(2,1)} %squeeze.59), calls=%async_computation.1 | async-start | bytes 524288 | tf_op jit(solution)/shard_map/all_to_all | solution.py:50
  60.4 20.6 %reduce-scatter.7.cloned.1.call-done = bf16[192,64]{1,0:T(8,128)(2,1)} async-done(((bf16[768,64]{1,0:T(8,128)(2,1)}), bf16[192,64]{1,0:T(8,128)(2,1)}) %reduce-scatter.7.cloned.1.call-update) | async-done | bytes 24592
  81.0 0.9 copy.62
  82.0 8.5 %all-gather = bf16[4,192,64]{1,2,0:T(8,128)(2,1)S(1)} all-gather(bf16[1,192,64]{1,2,0:T(8,128)(2,1)S(1)} %fusion.84), channel_id=1, replica_groups=mesh['head'=4,'pb'=8] {'head'}, dimensions={0}, use_global_device_ids=true | all-gather | bytes 122880 | tf_op jit(solution)/shard_map/all_gather | solution.py:108
  90.7 0.2 reshape.143
  90.9 0.2 multiply_reduce_fusion.2
  91.2 0.2 convolution_convert_fusion.4
  91.4 0.2 convolution_convert_fusion.5
  91.8 14.5 %all_gather.14 = bf16[512,384]{1,0:T(8,128)(2,1)S(1)} all-gather(bf16[64,384]{1,0:T(8,128)(2,1)S(1)} %pad_maximum_fusion.1), channel_id=1, replica_groups=mesh['head'=4,'pb'=8] {'pb'}, dimensions={0}, use_global_device_ids=true | all-gather | bytes 442368 | tf_op jit(solution)/shard_map/all_gather | solution.py:78
  106.5 0.2 convolution_convert_fusion.6
  107.0 0.4 fusion.96
  107.4 0.2 fusion.56
  107.7 0.3 fusion.39
  108.1 0.4 convolution_convert_fusion.1
  108.5 0.8 copy.63
  109.3 24.4 %reduce-scatter.9.cloned.1.call-done = bf16[192,64]{1,0:T(8,128)(2,1)} async-done(((bf16[768,64]{1,0:T(8,128)(2,1)}), bf16[192,64]{1,0:T(8,128)(2,1)}) %reduce-scatter.9.cloned.1.call-update) | async-done | bytes 24592
  133.8 0.9 copy.64
  134.7 8.5 %all-gather.1 = bf16[4,192,64]{1,2,0:T(8,128)(2,1)S(1)} all-gather(bf16[1,192,64]{1,2,0:T(8,128)(2,1)S(1)} %fusion.85), channel_id=1, replica_groups=mesh['head'=4,'pb'=8] {'head'}, dimensions={0}, use_global_device_ids=true | all-gather | bytes 122880 | tf_op jit(solution)/shard_map/all_gather | solution.py:108
  143.3 0.8 reshape.142
  (113 shorter events, 5.0 us)
Async XLA Ops:
  6.5 1.6 %copy-start = (bf16[2,128,512]{2,1,0:T(8,128)(2,1)S(1)}, bf16[2,128,512]{2,1,0:T(8,128)(2,1)}, u32[]{:S(2)}) copy-start(bf16[2,128,512]{2,1,0:T(8,128)(2,1)} %get-tuple-element.144) | copy-start | bytes 786436 | tf_op jit(solution)/shard_map/while
  8.2 0.9 copy-start.9
  10.8 1.0 copy-start.2
  12.1 1.6 %copy-start = (bf16[2,128,512]{2,1,0:T(8,128)(2,1)S(1)}, bf16[2,128,512]{2,1,0:T(8,128)(2,1)}, u32[]{:S(2)}) copy-start(bf16[2,128,512]{2,1,0:T(8,128)(2,1)} %get-tuple-element.144) | copy-start | bytes 786436 | tf_op jit(solution)/shard_map/while
  13.7 0.9 copy-start.9
  16.4 1.0 copy-start.2
  17.6 1.6 %copy-start = (bf16[2,128,512]{2,1,0:T(8,128)(2,1)S(1)}, bf16[2,128,512]{2,1,0:T(8,128)(2,1)}, u32[]{:S(2)}) copy-start(bf16[2,128,512]{2,1,0:T(8,128)(2,1)} %get-tuple-element.144) | copy-start | bytes 786436 | tf_op jit(solution)/shard_map/while
  19.3 0.9 copy-start.9
  21.9 1.0 copy-start.2
  23.2 1.6 %copy-start = (bf16[2,128,512]{2,1,0:T(8,128)(2,1)S(1)}, bf16[2,128,512]{2,1,0:T(8,128)(2,1)}, u32[]{:S(2)}) copy-start(bf16[2,128,512]{2,1,0:T(8,128)(2,1)} %get-tuple-element.144) | copy-start | bytes 786436 | tf_op jit(solution)/shard_map/while
  24.8 0.9 copy-start.9
  27.5 1.0 copy-start.2
  28.7 6.4 %copy-start.1 = (bf16[64,768]{1,0:T(8,128)(2,1)S(1)}, bf16[64,768]{1,0:T(8,128)(2,1)}, u32[]{:S(2)}) copy-start(bf16[64,768]{1,0:T(8,128)(2,1)} %param.14) | copy-start | bytes 294916
  28.8 6.7 %copy-start.4 = (bf16[2,768,192]{1,2,0:T(8,128)(2,1)S(1)}, bf16[2,768,192]{1,2,0:T(8,128)(2,1)}, u32[]{:S(2)}) copy-start(bf16[2,768,192]{1,2,0:T(8,128)(2,1)} %param.21) | copy-start | bytes 1769476
  28.8 7.0 %copy-start.5 = (bf16[2,768,192]{1,2,0:T(8,128)(2,1)S(1)}, bf16[2,768,192]{1,2,0:T(8,128)(2,1)}, u32[]{:S(2)}) copy-start(bf16[2,768,192]{1,2,0:T(8,128)(2,1)} %param.20) | copy-start | bytes 1769476
  29.0 22.1 %copy-start.6 = (bf16[2,768,192]{1,2,0:T(8,128)(2,1)S(1)}, bf16[2,768,192]{1,2,0:T(8,128)(2,1)}, u32[]{:S(2)}) copy-start(bf16[2,768,192]{1,2,0:T(8,128)(2,1)} %param.19) | copy-start | bytes 1769476
  29.9 21.7 %all-to-all-start = ((bf16[16,64,128]{2,1,0:T(8,128)(2,1)}), bf16[16,64,128]{2,1,0:T(8,128)(2,1)S(1)}, u32[]{:S(2)}, u32[]{:S(2)}) async-start(bf16[16,64,128]{2,1,0:T(8,128)(2,1)} %squeeze.53), calls=%async_computation | async-start | bytes 524288 | tf_op jit(solution)/shard_map/all_to_all | solution.py:50
  35.1 45.9 %reduce-scatter.7.cloned.1.call-start = ((), (), s32[]{:S(2)}) async-start(), calls=%async_computation.4 | async-start | bytes 245760
  35.5 16.2 %copy-start.3 = (s32[512]{0:T(512)S(1)}, s32[512]{0:T(512)}, u32[]{:S(2)}) copy-start(s32[512]{0:T(512)} %param.15) | copy-start | bytes 6148
  56.1 51.0 %all-to-all-start.1 = ((bf16[16,64,128]{2,1,0:T(8,128)(2,1)}), bf16[16,64,128]{2,1,0:T(8,128)(2,1)S(1)}, u32[]{:S(2)}, u32[]{:S(2)}) async-start(bf16[16,64,128]{2,1,0:T(8,128)(2,1)} %squeeze.59), calls=%async_computation.1 | async-start | bytes 524288 | tf_op jit(solution)/shard_map/all_to_all | solution.py:50
  60.3 73.5 %reduce-scatter.9.cloned.1.call-start = ((), (), s32[]{:S(2)}) async-start(), calls=%async_computation.5 | async-start | bytes 245760
  106.4 1.7 %copy-start.7 = (bf16[2,192,768]{2,1,0:T(8,128)(2,1)S(1)}, bf16[2,192,768]{2,1,0:T(8,128)(2,1)}, u32[]{:S(2)}) copy-start(bf16[2,192,768]{2,1,0:T(8,128)(2,1)} %param.23) | copy-start | bytes 1769476
  106.4 1.7 %copy-start.8 = (bf16[2,768,192]{1,2,0:T(8,128)(2,1)S(1)}, bf16[2,768,192]{1,2,0:T(8,128)(2,1)}, u32[]{:S(2)}) copy-start(bf16[2,768,192]{1,2,0:T(8,128)(2,1)} %param.22) | copy-start | bytes 1769476
Sparse Core Ops, SparseCore 0:
  55.1 25.8 reduce-scatter.6
  109.5 24.2 reduce-scatter.8
where the time goes:
time: 152 us; the launch traced here: 151 us
  blocking collectives  46.2 us (30%)
  waiting for transfers between devices  45.1 us (30%)
  matrix products  18.1 us (12%)
  local copies, waits for them, and re-layouts  14 us (9%)
  between operations  13.9 us (9%)
  starting transfers between devices  9.39 us (6%)
  other arithmetic  3.75 us (2%)
    unnamed x4, waiting for transfers between devices  45.1 us
    all_gather x2, blocking collectives, on_device(): every_key = lax.all_gather(packed, 'pb', axis=0, tiled=True)  29.2 us
    all_gather x2, blocking collectives, on_device(): lax.all_gather((own_features + query_real[:, None] * feature_share).astyp...  17 us
    all_to_all x2, starting transfers between devices, on_device(): lax.all_to_all(bias_local[layer_index], 'head', split_axis=0, concat_axis...  9.39 us
    dot_general x8, matrix products, transition(): jnp.dot(hidden, w_back, preferred_element_type=jnp.float32)  6.65 us
    dot_general x8, matrix products, transition(): mixed = jnp.dot(normed, w_updown, preferred_element_type=jnp.float32)  5.9 us
    dynamic_slice x8, local copies, waits for them, and re-layouts, on_device(): projected = lax.map(project, blocked)  5.33 us
    unnamed x19, local copies, waits for them, and re-layouts  4.22 us
  transfers between devices with their start and end apart: 4, of which 2 were waited for; matrix products, arithmetic and copies ran while one was open for 4% of the time, Pallas kernels for 0%

commit v1 on v0

--- a/solution.py
+++ b/solution.py
@@ -75,7 +75,14 @@
         packed = jnp.concatenate([key_proj, value_proj], axis=1)
         query_heads = queries.astype(jnp.float32).reshape(row_count, local_heads, HD)
         bias_now = layer_bias[layer_index]
-        every_key = lax.all_gather(packed, "pb", axis=0, tiled=True)
+        ring = [packed]
+        for hop in range(7):
+            ring.append(lax.ppermute(ring[-1], "pb", [(dev, (dev + 1) % 8) for dev in range(8)]))
+        every_key = jnp.roll(
+            jnp.concatenate(ring[::-1], axis=0),
+            (lax.axis_index("pb") + 1) * ring[0].shape[0],
+            axis=0,
+        )
         piece_len = every_key.shape[0]
         key_heads = (
             every_key[:, :local_width].astype(jnp.float32).reshape(piece_len, local_heads, HD)

time: 152 us -> 185 us (1.22)
  waiting for transfers between devices: 45.1 us -> 104 us
  blocking collectives: 46.2 us -> 17 us
  other arithmetic: 3.75 us -> 7.17 us
    ppermute x0 -> x14, waiting for transfers between devices: none -> 58.9 us  [on_device(): lax.ppermute(ring[-1], 'pb', [(dev, (dev + 1) % 8) for dev in range(8)])]
    all_gather x2 -> x0, blocking collectives: 29.2 us -> none  [on_device(): every_key = lax.all_gather(packed, 'pb', axis=0, tiled=True)]
    unnamed x19 -> x35, local copies, waits for them, and re-layouts: 4.22 us -> 4.38 us
  transfers between devices with their start and end apart: 4 -> 18, of which waited for: 2 -> 14; matrix products, arithmetic and copies ran while one was open for 4% -> 14% of each run, Pallas kernels for 0% -> 0%
where the time goes in v1:
time: 185 us; the launch traced here: 184 us
  waiting for transfers between devices  104 us (56%)
  matrix products  18.9 us (10%)
  blocking collectives  17 us (9%)
  local copies, waits for them, and re-layouts  14.2 us (8%)
  between operations  14 us (8%)
  starting transfers between devices  8.36 us (5%)
  other arithmetic  7.17 us (4%)
    ppermute x14, waiting for transfers between devices, on_device(): lax.ppermute(ring[-1], 'pb', [(dev, (dev + 1) % 8) for dev in range(8)])  58.9 us
    unnamed x4, waiting for transfers between devices  45.2 us
    all_gather x2, blocking collectives, on_device(): lax.all_gather((own_features + query_real[:, None] * feature_share).astyp...  17 us
    all_to_all x2, starting transfers between devices, on_device(): lax.all_to_all(bias_local[layer_index], 'head', split_axis=0, concat_axis...  7.6 us
    dot_general x8, matrix products, transition(): jnp.dot(hidden, w_back, preferred_element_type=jnp.float32)  6.51 us
    dot_general x8, matrix products, transition(): mixed = jnp.dot(normed, w_updown, preferred_element_type=jnp.float32)  5.88 us
    dynamic_slice x8, local copies, waits for them, and re-layouts, on_device(): projected = lax.map(project, blocked)  5.36 us
    unnamed x35, local copies, waits for them, and re-layouts  4.38 us
  transfers between devices with their start and end apart: 18, of which 14 were waited for; matrix products, arithmetic and copies ran while one was open for 14% of the time, Pallas kernels for 0%

profile of v1, /device:TPU:0, one launch (start us, length us, event | category | flops | bytes accessed | tf_op | source)
XLA Modules:
  0.0 184.3 jit_solution(10783967497559082110)
XLA Ops:
  6.5 1.0 convert_reduce_fusion.1
  7.6 1.1 multiply_reduce_fusion.3
  8.7 1.3 convolution_convert_fusion.8
  9.9 1.3 convolution_convert_fusion.9
  11.3 0.5 collective-permute-start
  11.8 5.8 %collective-permute-done = bf16[64,384]{1,0:T(8,128)(2,1)S(1)} collective-permute-done((bf16[64,384]{1,0:T(8,128)(2,1)S(1)}, bf16[64,384]{1,0:T(8,128)(2,1)S(1)}, u32[]{:S(2)}, u32[]{:S(2)}) %collective-permute-start) | collective-permute-done | bytes 49184 | tf_op jit(solution)/shard_map/ppermute | solution.py:80
  17.6 5.3 %collective-permute-done.1 = bf16[64,384]{1,0:T(8,128)(2,1)S(1)} collective-permute-done((bf16[64,384]{1,0:T(8,128)(2,1)S(1)}, bf16[64,384]{1,0:T(8,128)(2,1)S(1)}, u32[]{:S(2)}, u32[]{:S(2)}) %collective-permute-start.1) | collective-permute-done | bytes 49184 | tf_op jit(solution)/shard_map/ppermute | solution.py:80
  23.0 5.3 %collective-permute-done.2 = bf16[64,384]{1,0:T(8,128)(2,1)S(1)} collective-permute-done((bf16[64,384]{1,0:T(8,128)(2,1)S(1)}, bf16[64,384]{1,0:T(8,128)(2,1)S(1)}, u32[]{:S(2)}, u32[]{:S(2)}) %collective-permute-start.2) | collective-permute-done | bytes 49184 | tf_op jit(solution)/shard_map/ppermute | solution.py:80
  28.3 22.1 %while.10 = (s32[]{:T(128)}, bf16[4,32,2048]{2,1,0:T(8,128)(2,1)S(1)}, bf16[4,2048,128]{2,1,0:T(8,128)(2,1)}, bf16[2,128,512]{2,1,0:T(8,128)(2,1)}, bf16[2,256,1...) while((s32[]{:T(128)}, bf16[4,32,2048]{2,1,0:T(8,128)(2,1)S(1)}, ...), condition=%wide.region_9.11_spmd, body=%wide.region_2.10_spmd.sunk | while | flops 836573184 | bytes 30671024 | solution.py:46
  28.3 1.1 constant_dynamic-slice_fusion.2
  29.9 0.7 fusion.125
  30.8 0.8 fusion.126
  31.8 0.7 fusion.127
  32.5 0.8 fusion.128
  33.5 0.2 fusion.129
  33.8 1.1 constant_dynamic-slice_fusion.2
  35.4 0.7 fusion.125
  36.3 0.8 fusion.126
  37.3 0.7 fusion.127
  38.1 0.8 fusion.128
  39.0 0.2 fusion.129
  39.3 1.1 constant_dynamic-slice_fusion.2
  41.0 0.7 fusion.125
  41.9 0.8 fusion.126
  42.8 0.7 fusion.127
  43.6 0.8 fusion.128
  44.6 0.2 fusion.129
  44.8 1.1 constant_dynamic-slice_fusion.2
  46.5 0.7 fusion.125
  47.4 0.8 fusion.126
  48.4 0.7 fusion.127
  49.1 0.8 fusion.128
  50.1 0.2 fusion.129
  50.7 0.9 squeeze.53
  51.6 4.2 %all-to-all-start = ((bf16[16,64,128]{2,1,0:T(8,128)(2,1)}), bf16[16,64,128]{2,1,0:T(8,128)(2,1)S(1)}, u32[]{:S(2)}, u32[]{:S(2)}) async-start(bf16[16,64,128]{2,1,0:T(8,128)(2,1)} %squeeze.53), calls=%async_computation | async-start | bytes 524288 | tf_op jit(solution)/shard_map/all_to_all | solution.py:50
  56.1 5.0 %collective-permute-done.5 = bf16[64,384]{1,0:T(8,128)(2,1)S(1)} collective-permute-done((bf16[64,384]{1,0:T(8,128)(2,1)S(1)}, bf16[64,384]{1,0:T(8,128)(2,1)S(1)}, u32[]{:S(2)}, u32[]{:S(2)}) %collective-permute-start.5) | collective-permute-done | bytes 49184 | tf_op jit(solution)/shard_map/ppermute | solution.py:80
  61.3 5.2 %collective-permute-done.6 = bf16[64,384]{1,0:T(8,128)(2,1)S(1)} collective-permute-done((bf16[64,384]{1,0:T(8,128)(2,1)S(1)}, bf16[64,384]{1,0:T(8,128)(2,1)S(1)}, u32[]{:S(2)}, u32[]{:S(2)}) %collective-permute-start.6) | collective-permute-done | bytes 49184 | tf_op jit(solution)/shard_map/ppermute | solution.py:80
  66.6 0.7 fusion.58
  67.8 0.4 fusion.97
  68.4 0.3 fusion.40
  68.9 0.5 convolution_convert_fusion.2
  69.3 0.8 copy.61
  70.3 23.0 %reduce-scatter.7.cloned.1.call-done = bf16[192,64]{1,0:T(8,128)(2,1)} async-done(((bf16[768,64]{1,0:T(8,128)(2,1)}), bf16[192,64]{1,0:T(8,128)(2,1)}) %reduce-scatter.7.cloned.1.call-update) | async-done | bytes 24592
  93.2 0.9 copy.62
  94.2 8.5 %all-gather = bf16[4,192,64]{1,2,0:T(8,128)(2,1)S(1)} all-gather(bf16[1,192,64]{1,2,0:T(8,128)(2,1)S(1)} %fusion.86), channel_id=1, replica_groups=mesh['head'=4,'pb'=8] {'head'}, dimensions={0}, use_global_device_ids=true | all-gather | bytes 122880 | tf_op jit(solution)/shard_map/all_gather | solution.py:115
  104.0 5.3 %collective-permute-done.7 = bf16[64,384]{1,0:T(8,128)(2,1)S(1)} collective-permute-done((bf16[64,384]{1,0:T(8,128)(2,1)S(1)}, bf16[64,384]{1,0:T(8,128)(2,1)S(1)}, u32[]{:S(2)}, u32[]{:S(2)}) %collective-permute-start.7) | collective-permute-done | bytes 49184 | tf_op jit(solution)/shard_map/ppermute | solution.py:80
  109.3 5.3 %collective-permute-done.8 = bf16[64,384]{1,0:T(8,128)(2,1)S(1)} collective-permute-done((bf16[64,384]{1,0:T(8,128)(2,1)S(1)}, bf16[64,384]{1,0:T(8,128)(2,1)S(1)}, u32[]{:S(2)}, u32[]{:S(2)}) %collective-permute-start.8) | collective-permute-done | bytes 49184 | tf_op jit(solution)/shard_map/ppermute | solution.py:80
  114.7 5.3 %collective-permute-done.9 = bf16[64,384]{1,0:T(8,128)(2,1)S(1)} collective-permute-done((bf16[64,384]{1,0:T(8,128)(2,1)S(1)}, bf16[64,384]{1,0:T(8,128)(2,1)S(1)}, u32[]{:S(2)}, u32[]{:S(2)}) %collective-permute-start.9) | collective-permute-done | bytes 49184 | tf_op jit(solution)/shard_map/ppermute | solution.py:80
  120.0 5.3 %collective-permute-done.10 = bf16[64,384]{1,0:T(8,128)(2,1)S(1)} collective-permute-done((bf16[64,384]{1,0:T(8,128)(2,1)S(1)}, bf16[64,384]{1,0:T(8,128)(2,1)S(1)}, u32[]{:S(2)}, u32[]{:S(2)}) %collective-permute-start.10) | collective-permute-done | bytes 49184 | tf_op jit(solution)/shard_map/ppermute | solution.py:80
  125.3 5.3 %collective-permute-done.11 = bf16[64,384]{1,0:T(8,128)(2,1)S(1)} collective-permute-done((bf16[64,384]{1,0:T(8,128)(2,1)S(1)}, bf16[64,384]{1,0:T(8,128)(2,1)S(1)}, u32[]{:S(2)}, u32[]{:S(2)}) %collective-permute-start.11) | collective-permute-done | bytes 49184 | tf_op jit(solution)/shard_map/ppermute | solution.py:80
  130.8 0.9 squeeze.59
  131.7 3.4 %all-to-all-start.1 = ((bf16[16,64,128]{2,1,0:T(8,128)(2,1)}), bf16[16,64,128]{2,1,0:T(8,128)(2,1)S(1)}, u32[]{:S(2)}, u32[]{:S(2)}) async-start(bf16[16,64,128]{2,1,0:T(8,128)(2,1)} %squeeze.59), calls=%async_computation.1 | async-start | bytes 524288 | tf_op jit(solution)/shard_map/all_to_all | solution.py:50
  135.1 0.8 collective-permute-done.12
  136.3 5.0 %collective-permute-done.13 = bf16[64,384]{1,0:T(8,128)(2,1)S(1)} collective-permute-done((bf16[64,384]{1,0:T(8,128)(2,1)S(1)}, bf16[64,384]{1,0:T(8,128)(2,1)S(1)}, u32[]{:S(2)}, u32[]{:S(2)}) %collective-permute-start.13) | collective-permute-done | bytes 49184 | tf_op jit(solution)/shard_map/ppermute | solution.py:80
  141.4 0.7 fusion.57
  142.6 0.4 fusion.98
  143.0 0.2 fusion.56
  143.2 0.3 fusion.39
  143.6 0.4 convolution_convert_fusion.1
  144.0 0.8 copy.63
  144.9 22.3 %reduce-scatter.9.cloned.1.call-done = bf16[192,64]{1,0:T(8,128)(2,1)} async-done(((bf16[768,64]{1,0:T(8,128)(2,1)}), bf16[192,64]{1,0:T(8,128)(2,1)}) %reduce-scatter.9.cloned.1.call-update) | async-done | bytes 24592
  167.1 0.9 copy.64
  168.1 8.5 %all-gather.1 = bf16[4,192,64]{1,2,0:T(8,128)(2,1)S(1)} all-gather(bf16[1,192,64]{1,2,0:T(8,128)(2,1)S(1)} %fusion.87), channel_id=1, replica_groups=mesh['head'=4,'pb'=8] {'head'}, dimensions={0}, use_global_device_ids=true | all-gather | bytes 122880 | tf_op jit(solution)/shard_map/all_gather | solution.py:115
  176.7 0.8 reshape.142
  (159 shorter events, 8.3 us)
Async XLA Ops:
  11.3 6.3 %collective-permute-start = (bf16[64,384]{1,0:T(8,128)(2,1)S(1)}, bf16[64,384]{1,0:T(8,128)(2,1)S(1)}, u32[]{:S(2)}, u32[]{:S(2)}) collective-permute-start(bf16[64,384]{1,0:T(8,128)(2,1)S(1)} %pad_maximum_fusion), channel_id=1, source_target_pairs={{0,1},{1,2},{2,3},{3,4},{4,5},{5,6},{6,7},{7,0},{8,9},{9,10},{10,1... | collective-permute-start | bytes 147464 | tf_op jit(solution)/shard_map/ppermute | solution.py:80
  17.6 5.3 %collective-permute-start.1 = (bf16[64,384]{1,0:T(8,128)(2,1)S(1)}, bf16[64,384]{1,0:T(8,128)(2,1)S(1)}, u32[]{:S(2)}, u32[]{:S(2)}) collective-permute-start(bf16[64,384]{1,0:T(8,128)(2,1)S(1)} %collective-permute-done), channel_id=1, source_target_pairs={{0,1},{1,2},{2,3},{3,4},{4,5},{5,6},{6,7},{7,0},{8,9},{9,10},{10,1... | collective-permute-start | bytes 147464 | tf_op jit(solution)/shard_map/ppermute | solution.py:80
  22.9 5.3 %collective-permute-start.2 = (bf16[64,384]{1,0:T(8,128)(2,1)S(1)}, bf16[64,384]{1,0:T(8,128)(2,1)S(1)}, u32[]{:S(2)}, u32[]{:S(2)}) collective-permute-start(bf16[64,384]{1,0:T(8,128)(2,1)S(1)} %collective-permute-done.1), channel_id=1, source_target_pairs={{0,1},{1,2},{2,3},{3,4},{4,5},{5,6},{6,7},{7,0},{8,9},{9,10},{10,1... | collective-permute-start | bytes 147464 | tf_op jit(solution)/shard_map/ppermute | solution.py:80
  28.3 22.1 %collective-permute-start.3 = (bf16[64,384]{1,0:T(8,128)(2,1)S(1)}, bf16[64,384]{1,0:T(8,128)(2,1)S(1)}, u32[]{:S(2)}, u32[]{:S(2)}) collective-permute-start(bf16[64,384]{1,0:T(8,128)(2,1)S(1)} %collective-permute-done.2), channel_id=1, source_target_pairs={{0,1},{1,2},{2,3},{3,4},{4,5},{5,6},{6,7},{7,0},{8,9},{9,10},{10,1... | collective-permute-start | bytes 147464 | tf_op jit(solution)/shard_map/ppermute | solution.py:80
  28.3 1.6 copy-start
  29.9 0.9 copy-start.10
  32.5 1.0 copy-start.2
  33.8 1.6 copy-start
  35.4 0.9 copy-start.10
  38.1 1.0 copy-start.2
  39.3 1.6 copy-start
  40.9 0.9 copy-start.10
  43.6 1.0 copy-start.2
  44.8 1.6 copy-start
  46.5 0.9 copy-start.10
  49.1 1.0 copy-start.2
  50.3 5.5 %copy-start.1 = (bf16[64,768]{1,0:T(8,128)(2,1)S(1)}, bf16[64,768]{1,0:T(8,128)(2,1)}, u32[]{:S(2)}) copy-start(bf16[64,768]{1,0:T(8,128)(2,1)} %param.16) | copy-start | bytes 294916
  50.3 5.5 %copy-start.6 = (bf16[2,768,192]{1,2,0:T(8,128)(2,1)S(1)}, bf16[2,768,192]{1,2,0:T(8,128)(2,1)}, u32[]{:S(2)}) copy-start(bf16[2,768,192]{1,2,0:T(8,128)(2,1)} %param.21) | copy-start | bytes 1769476
  50.4 10.8 %copy-start.3 = (s32[512]{0:T(512)S(1)}, s32[512]{0:T(512)}, u32[]{:S(2)}) copy-start(s32[512]{0:T(512)} %param.17) | copy-start | bytes 6148
  50.4 5.4 %collective-permute-start.4 = (bf16[64,384]{1,0:T(8,128)(2,1)S(1)}, bf16[64,384]{1,0:T(8,128)(2,1)S(1)}, u32[]{:S(2)}, u32[]{:S(2)}) collective-permute-start(bf16[64,384]{1,0:T(8,128)(2,1)S(1)} %collective-permute-done.3), channel_id=1, source_target_pairs={{0,1},{1,2},{2,3},{3,4},{4,5},{5,6},{6,7},{7,0},{8,9},{9,10},{10,1... | collective-permute-start | bytes 147464 | tf_op jit(solution)/shard_map/ppermute | solution.py:80
  51.6 16.3 %all-to-all-start = ((bf16[16,64,128]{2,1,0:T(8,128)(2,1)}), bf16[16,64,128]{2,1,0:T(8,128)(2,1)S(1)}, u32[]{:S(2)}, u32[]{:S(2)}) async-start(bf16[16,64,128]{2,1,0:T(8,128)(2,1)} %squeeze.53), calls=%async_computation | async-start | bytes 524288 | tf_op jit(solution)/shard_map/all_to_all | solution.py:50
  55.8 37.5 %reduce-scatter.7.cloned.1.call-start = ((), (), s32[]{:S(2)}) async-start(), calls=%async_computation.4 | async-start | bytes 245760
  55.8 5.4 %collective-permute-start.5 = (bf16[64,384]{1,0:T(8,128)(2,1)S(1)}, bf16[64,384]{1,0:T(8,128)(2,1)S(1)}, u32[]{:S(2)}, u32[]{:S(2)}) collective-permute-start(bf16[64,384]{1,0:T(8,128)(2,1)S(1)} %collective-permute-done.4), channel_id=1, source_target_pairs={{0,1},{1,2},{2,3},{3,4},{4,5},{5,6},{6,7},{7,0},{8,9},{9,10},{10,1... | collective-permute-start | bytes 147464 | tf_op jit(solution)/shard_map/ppermute | solution.py:80
  61.1 5.3 %collective-permute-start.6 = (bf16[64,384]{1,0:T(8,128)(2,1)S(1)}, bf16[64,384]{1,0:T(8,128)(2,1)S(1)}, u32[]{:S(2)}, u32[]{:S(2)}) collective-permute-start(bf16[64,384]{1,0:T(8,128)(2,1)S(1)} %collective-permute-done.5), channel_id=1, source_target_pairs={{0,1},{1,2},{2,3},{3,4},{4,5},{5,6},{6,7},{7,0},{8,9},{9,10},{10,1... | collective-permute-start | bytes 147464 | tf_op jit(solution)/shard_map/ppermute | solution.py:80
  67.4 1.5 copy-start.7
  67.4 1.5 copy-start.8
  68.8 34.7 %copy-start.4 = (bf16[2,768,192]{1,2,0:T(8,128)(2,1)S(1)}, bf16[2,768,192]{1,2,0:T(8,128)(2,1)}, u32[]{:S(2)}) copy-start(bf16[2,768,192]{1,2,0:T(8,128)(2,1)} %param.23) | copy-start | bytes 1769476
  68.9 34.8 %copy-start.5 = (bf16[2,768,192]{1,2,0:T(8,128)(2,1)S(1)}, bf16[2,768,192]{1,2,0:T(8,128)(2,1)}, u32[]{:S(2)}) copy-start(bf16[2,768,192]{1,2,0:T(8,128)(2,1)} %param.22) | copy-start | bytes 1769476
  104.0 5.3 %collective-permute-start.7 = (bf16[64,384]{1,0:T(8,128)(2,1)S(1)}, bf16[64,384]{1,0:T(8,128)(2,1)S(1)}, u32[]{:S(2)}, u32[]{:S(2)}) collective-permute-start(bf16[64,384]{1,0:T(8,128)(2,1)S(1)} %pad_maximum_fusion.1), channel_id=1, source_target_pairs={{0,1},{1,2},{2,3},{3,4},{4,5},{5,6},{6,7},{7,0},{8,9},{9,10},{10,1... | collective-permute-start | bytes 147464 | tf_op jit(solution)/shard_map/ppermute | solution.py:80
  109.3 5.3 %collective-permute-start.8 = (bf16[64,384]{1,0:T(8,128)(2,1)S(1)}, bf16[64,384]{1,0:T(8,128)(2,1)S(1)}, u32[]{:S(2)}, u32[]{:S(2)}) collective-permute-start(bf16[64,384]{1,0:T(8,128)(2,1)S(1)} %collective-permute-done.7), channel_id=1, source_target_pairs={{0,1},{1,2},{2,3},{3,4},{4,5},{5,6},{6,7},{7,0},{8,9},{9,10},{10,1... | collective-permute-start | bytes 147464 | tf_op jit(solution)/shard_map/ppermute | solution.py:80
  114.7 5.3 %collective-permute-start.9 = (bf16[64,384]{1,0:T(8,128)(2,1)S(1)}, bf16[64,384]{1,0:T(8,128)(2,1)S(1)}, u32[]{:S(2)}, u32[]{:S(2)}) collective-permute-start(bf16[64,384]{1,0:T(8,128)(2,1)S(1)} %collective-permute-done.8), channel_id=1, source_target_pairs={{0,1},{1,2},{2,3},{3,4},{4,5},{5,6},{6,7},{7,0},{8,9},{9,10},{10,1... | collective-permute-start | bytes 147464 | tf_op jit(solution)/shard_map/ppermute | solution.py:80
  120.0 5.3 %collective-permute-start.10 = (bf16[64,384]{1,0:T(8,128)(2,1)S(1)}, bf16[64,384]{1,0:T(8,128)(2,1)S(1)}, u32[]{:S(2)}, u32[]{:S(2)}) collective-permute-start(bf16[64,384]{1,0:T(8,128)(2,1)S(1)} %collective-permute-done.9), channel_id=1, source_target_pairs={{0,1},{1,2},{2,3},{3,4},{4,5},{5,6},{6,7},{7,0},{8,9},{9,10},{10,1... | collective-permute-start | bytes 147464 | tf_op jit(solution)/shard_map/ppermute | solution.py:80
  125.3 5.3 %collective-permute-start.11 = (bf16[64,384]{1,0:T(8,128)(2,1)S(1)}, bf16[64,384]{1,0:T(8,128)(2,1)S(1)}, u32[]{:S(2)}, u32[]{:S(2)}) collective-permute-start(bf16[64,384]{1,0:T(8,128)(2,1)S(1)} %collective-permute-done.10), channel_id=1, source_target_pairs={{0,1},{1,2},{2,3},{3,4},{4,5},{5,6},{6,7},{7,0},{8,9},{9,10},{10,1... | collective-permute-start | bytes 147464 | tf_op jit(solution)/shard_map/ppermute | solution.py:80
  130.6 5.3 %collective-permute-start.12 = (bf16[64,384]{1,0:T(8,128)(2,1)S(1)}, bf16[64,384]{1,0:T(8,128)(2,1)S(1)}, u32[]{:S(2)}, u32[]{:S(2)}) collective-permute-start(bf16[64,384]{1,0:T(8,128)(2,1)S(1)} %collective-permute-done.11), channel_id=1, source_target_pairs={{0,1},{1,2},{2,3},{3,4},{4,5},{5,6},{6,7},{7,0},{8,9},{9,10},{10,1... | collective-permute-start | bytes 147464 | tf_op jit(solution)/shard_map/ppermute | solution.py:80
  131.7 10.9 %all-to-all-start.1 = ((bf16[16,64,128]{2,1,0:T(8,128)(2,1)}), bf16[16,64,128]{2,1,0:T(8,128)(2,1)S(1)}, u32[]{:S(2)}, u32[]{:S(2)}) async-start(bf16[16,64,128]{2,1,0:T(8,128)(2,1)} %squeeze.59), calls=%async_computation.1 | async-start | bytes 524288 | tf_op jit(solution)/shard_map/all_to_all | solution.py:50
  135.1 32.0 %reduce-scatter.9.cloned.1.call-start = ((), (), s32[]{:S(2)}) async-start(), calls=%async_computation.5 | async-start | bytes 245760
  135.9 5.3 %collective-permute-start.13 = (bf16[64,384]{1,0:T(8,128)(2,1)S(1)}, bf16[64,384]{1,0:T(8,128)(2,1)S(1)}, u32[]{:S(2)}, u32[]{:S(2)}) collective-permute-start(bf16[64,384]{1,0:T(8,128)(2,1)S(1)} %collective-permute-done.12), channel_id=1, source_target_pairs={{0,1},{1,2},{2,3},{3,4},{4,5},{5,6},{6,7},{7,0},{8,9},{9,10},{10,1... | collective-permute-start | bytes 147464 | tf_op jit(solution)/shard_map/ppermute | solution.py:80
  142.2 1.4 copy-start.9
Sparse Core Ops, SparseCore 0:
  70.3 22.8 reduce-scatter.6
  145.0 22.0 reduce-scatter.8
